TPU v7x, 128 devices: a whole 4x4x4 slice. The times are simulated.
128 devices in a mesh: pipe: 8 (over y, core), expert: 16 (over z, x).
Axes of the slice: x: 4, y: 4, z: 4, core: 2. Of those that a mesh axis runs over, the one named last changes fastest.
Arguments:
- boundary_grad: bfloat16 [8, 4096, 3584], P('pipe', 'expert'), may hold values from -6 to 6
- route_ids: int32 [8, 4096, 8], P('pipe', 'expert'), may hold values from 0 to 255, as said below
- route_probs: bfloat16 [8, 4096, 8], P('pipe', 'expert'), may hold values from 0.049804688 to 1
- saved_preact: bfloat16 [8, 16, 1024, 2048], P('pipe', 'expert'), may hold values from -6 to 6
- down_weight: bfloat16 [8, 16, 1024, 3584], P('pipe', 'expert'), may hold values from -0.046875 to 0.046875
Outputs:
- preact_grad: bfloat16 [8, 16, 1024, 2048], P('pipe', 'expert')
- down_grad: bfloat16 [8, 16, 1024, 3584], P('pipe', 'expert')
- prob_grad: float32 [8, 4096, 8], P('pipe', 'expert')
Inputs may be any that keep to these rules, and one draw needn't show every extreme that they name: `route_ids`: each token names 8 different experts. Window experts are 0 to 15. In each aligned block of 256 tokens of a section (the tokens of one device) each window expert is named by at most 64 tokens, and in every section one window expert is named by exactly 64 tokens of every block.
All inputs are finite; a program needn't handle non-finite values.
Results may differ from a plain program's by a relative error of at most 0.0057.
Values may be sent and summed in bfloat16 or wider, within the bound.
A program may use at most 192 MiB of HBM per device.

v0:
```python
import jax
import jax.numpy as jnp
from jax import lax
from jax.sharding import PartitionSpec as P


def passed_along(block, axis, distance):
    devices = range(lax.axis_size(axis))
    route = [((i - distance) % len(devices), i) for i in devices]
    return lax.ppermute(block, axis, route)


def activation(gate_up):
    half_width = gate_up.shape[1] // 2
    gate_pre = gate_up[:, :half_width].astype(jnp.float32)
    up_pre = gate_up[:, half_width:].astype(jnp.float32)
    sigmoid_gate = jax.nn.sigmoid(gate_pre)
    return (gate_pre, up_pre, sigmoid_gate)


def hidden_rows(gate_up):
    gate_pre, up_pre, sigmoid_gate = activation(gate_up)
    return (gate_pre * sigmoid_gate * up_pre).astype(jnp.bfloat16)


def prob_terms(gate_up, row_grad, weight):
    expert_out = jnp.dot(hidden_rows(gate_up), weight, preferred_element_type=jnp.float32)
    return jnp.sum(row_grad.astype(jnp.float32) * expert_out, axis=1)


def weight_terms(gate_up, weighted):
    return lax.dot_general(
        hidden_rows(gate_up), weighted, (((0,), (0,)), ((), ())), preferred_element_type=jnp.float32
    )


def input_terms(gate_up, weighted, weight):
    gate_pre, up_pre, sigmoid_gate = activation(gate_up)
    hidden_grad = lax.dot_general(
        weighted, weight, (((1,), (1,)), ((), ())), preferred_element_type=jnp.float32
    )
    gate_grad = hidden_grad * up_pre * sigmoid_gate * (1.0 + gate_pre * (1.0 - sigmoid_gate))
    up_grad = hidden_grad * (gate_pre * sigmoid_gate)
    return jnp.concatenate([gate_grad, up_grad], axis=1).astype(jnp.bfloat16)


def on_device(boundary_grad, route_ids, route_probs, saved_preact, down_weight):
    experts = lax.axis_size("expert")
    cap_rows = saved_preact.shape[2] // experts
    slot_total = saved_preact.shape[2]
    out_grad = passed_along(boundary_grad, "pipe", -1)[0]
    routes = route_ids[0]
    probs = route_probs[0].astype(jnp.float32)
    expert_iota = jnp.arange(experts, dtype=jnp.int32)
    route_hits = routes[:, :, None] == expert_iota[None, None, :]
    member = jnp.sum(route_hits.astype(jnp.int32), axis=1)
    slot_rank = jnp.cumsum(member, axis=0) - 1
    slot_iota = jnp.arange(cap_rows, dtype=jnp.int32)
    placed = (member.T[:, None, :] == 1) & (slot_rank.T[:, None, :] == slot_iota[None, :, None])
    send_rows = jnp.einsum(
        "ert,td->erd", placed.astype(jnp.bfloat16), out_grad, preferred_element_type=jnp.float32
    ).astype(jnp.bfloat16)
    token_prob = jnp.sum(jnp.where(route_hits, probs[:, :, None], 0.0), axis=1)
    send_prob = jnp.sum(jnp.where(placed, token_prob.T[:, None, :], 0.0), axis=2).astype(
        jnp.bfloat16
    )
    recv_rows, recv_prob = (
        lax.all_to_all(send_rows, "expert", split_axis=0, concat_axis=0, tiled=True),
        lax.all_to_all(send_prob, "expert", split_axis=0, concat_axis=0, tiled=True),
    )
    row_grad = recv_rows.reshape(slot_total, recv_rows.shape[2])
    row_prob = recv_prob.reshape(slot_total).astype(jnp.float32)
    weighted = (row_prob[:, None] * row_grad.astype(jnp.float32)).astype(jnp.bfloat16)
    gate_up = saved_preact[0, 0]
    weight = down_weight[0, 0]
    block_rows = 512
    preact_parts = []
    prob_parts = []
    weight_grad = jnp.zeros(weight.shape, jnp.float32)
    for first_row in range(0, slot_total, block_rows):
        gate_block = gate_up[first_row : first_row + block_rows]
        weighted_block = weighted[first_row : first_row + block_rows]
        prob_parts.append(
            prob_terms(gate_block, row_grad[first_row : first_row + block_rows], weight)
        )
        weight_grad = weight_grad + weight_terms(gate_block, weighted_block)
        preact_parts.append(input_terms(gate_block, weighted_block, weight))
    preact_slots = jnp.concatenate(preact_parts, axis=0)
    prob_slots = jnp.concatenate(prob_parts, axis=0)
    back = lax.all_to_all(
        prob_slots.reshape(experts, cap_rows), "expert", split_axis=0, concat_axis=0, tiled=True
    )
    token_grad = jnp.sum(jnp.where(placed, back[:, :, None], 0.0), axis=1)
    prob_grad = jnp.sum(jnp.where(route_hits, token_grad.T[:, None, :], 0.0), axis=2)
    return (preact_slots[None, None], weight_grad.astype(jnp.bfloat16)[None, None], prob_grad[None])


def solution(mesh):
    placed = (
        P("pipe", "expert", None),
        P("pipe", "expert", None),
        P("pipe", "expert", None),
        P("pipe", "expert", None, None),
        P("pipe", "expert", None, None),
    )
    return jax.shard_map(
        on_device,
        mesh=mesh,
        in_specs=placed,
        out_specs=(
            P("pipe", "expert", None, None),
            P("pipe", "expert", None, None),
            P("pipe", "expert", None),
        ),
        check_vma=False,
    )
```

profile of v0, /device:TPU:1, one launch (start us, length us, event | category | flops | bytes accessed | tf_op | source)
XLA Modules:
  0.0 233.2 jit_solution(4658883146137026888)
XLA Ops:
  0.6 1.4 collective-permute-start
  2.0 0.7 convert_reduce_fusion
  2.8 0.6 reduce-window.6
  3.3 0.2 slice_reduce_fusion
  3.6 0.1 copy_bitcast_fusion
  3.7 20.8 %collective-permute-done = bf16[1,256,3584]{2,1,0:T(8,128)(2,1)S(1)} collective-permute-done((bf16[1,256,3584]{2,1,0:T(8,128)(2,1)}, bf16[1,256,3584]{2,1,0:T(8,128)(2,1)S(1)}, u32[]{:S(2)}, u32[]{:S(2)}) %collective-permute-start) | collective-permute-done | bytes 1835040 | tf_op jit(solution)/shard_map/ppermute | solution.py:10
  24.4 5.1 %convolution_convert_fusion = bf16[16,64,3584]{2,1,0:T(8,128)(2,1)} fusion(bf16[1,256,3584]{2,1,0:T(8,128)(2,1)S(1)} %collective-permute-done, s32[16,256]{1,0:T(8,128)S(1)} %copy_bitcast_fusion, pred[16,256]{1,0:T(8,128)(4,1)S(1)} %bitcast_compare_fusion), kind=kOutput, calls=%fused_computation.3 | convolution fusion | flops 1883242496 | bytes 9195520 | tf_op jit(solution)/shard_map/ert,td->erd/dot_general | solution.py:60
  29.6 0.0 copy-start.3
  29.6 7.8 %all-to-all-start.1 = ((bf16[16,64,3584]{2,1,0:T(8,128)(2,1)}), bf16[16,64,3584]{2,1,0:T(8,128)(2,1)}, u32[]{:S(2)}, u32[]{:S(2)}) async-start(bf16[16,64,3584]{2,1,0:T(8,128)(2,1)} %convolution_convert_fusion), calls=%async_computation.1 | async-start | bytes 14680064 | tf_op jit(solution)/shard_map/all_to_all | solution.py:68
  37.3 0.0 copy-done.3
  37.4 4.1 %slice_bitcast_fusion.1 = (bf16[512,2048]{1,0:T(8,128)(2,1)}, bf16[512,2048]{1,0:T(8,128)(2,1)S(1)}) fusion(bf16[1,1,1024,2048]{3,2,1,0:T(8,128)(2,1)} %param.8), kind=kLoop, calls=%fused_computation.52 | loop fusion | bytes 8388608 | tf_op jit(solution)/shard_map/slice | solution.py:81
  41.5 102.7 %all-to-all-done.1 = bf16[16,64,3584]{2,1,0:T(8,128)(2,1)} async-done(((bf16[16,64,3584]{2,1,0:T(8,128)(2,1)}), bf16[16,64,3584]{2,1,0:T(8,128)(2,1)}, u32[]{:S(2)}, u32[]{:S(2)}) %all-to-all-start.1) | async-done | bytes 7340064 | tf_op jit(solution)/shard_map/all_to_all | solution.py:68
  144.2 0.0 copy-start
  144.2 5.8 %fusion.50 = (bf16[8,64,3584]{2,1,0:T(8,128)(2,1)S(1)}, bf16[8,64,3584]{2,1,0:T(8,128)(2,1)}) fusion(bf16[16,64,3584]{2,1,0:T(8,128)(2,1)} %all-to-all-done.1), kind=kLoop, calls=%fused_computation.73 | loop fusion | bytes 14680064 | tf_op jit(solution)/shard_map/slice | solution.py:84
  150.0 0.0 copy-done
  150.0 7.7 %fusion.2 = f32[512]{0:T(512)S(1)} fusion(bf16[8,64,3584]{2,1,0:T(8,128)(2,1)S(1)} %get-tuple-element.5, bf16[1,1,1024,3584]{3,2,1,0:T(8,128)(2,1)} %param.9, bf16[512,2048]{1,0:T(8,128)(2,1)S(1)} %copy-done), kind=kOutput, calls=%fused_computation.7 | convolution fusion | flops 3767795200 | bytes 13109248 | tf_op jit(solution)/shard_map/dot_general | solution.py:27
  157.6 0.1 concatenate.22
  157.7 0.0 copy-start.2
  157.7 8.1 %fusion.1 = f32[512]{0:T(512)S(1)} fusion(bf16[8,64,3584]{2,1,0:T(8,128)(2,1)} %get-tuple-element.6, bf16[1,1,1024,3584]{3,2,1,0:T(8,128)(2,1)} %param.9, bf16[512,2048]{1,0:T(8,128)(2,1)S(1)} %get-tuple-element.12), kind=kOutput, calls=%fused_computation.5 | convolution fusion | flops 3767795200 | bytes 13109248 | tf_op jit(solution)/shard_map/dot_general | solution.py:27
  165.8 0.1 concatenate.23
  165.9 0.6 pad_maximum_fusion
  166.5 5.2 %all-to-all-start.2 = ((f32[16,1,64]{2,1,0:T(1,128)}), f32[16,1,64]{2,1,0:T(1,128)S(1)}, u32[]{:S(2)}, u32[]{:S(2)}) async-start(f32[16,1,64]{2,1,0:T(1,128)} %bitcast.15), calls=%async_computation.2 | async-start | bytes 16384 | tf_op jit(solution)/shard_map/all_to_all | solution.py:90
  171.8 0.0 copy-done.2
  171.8 6.3 %all-to-all-done.2 = f32[16,1,64]{2,1,0:T(1,128)S(1)} async-done(((f32[16,1,64]{2,1,0:T(1,128)}), f32[16,1,64]{2,1,0:T(1,128)S(1)}, u32[]{:S(2)}, u32[]{:S(2)}) %all-to-all-start.2) | async-done | bytes 4128 | tf_op jit(solution)/shard_map/all_to_all | solution.py:90
  178.1 0.6 select_reduce_fusion
  178.7 0.6 copy.27
  179.3 3.7 %all-to-all-start = ((bf16[16,1,64]{2,1,0:T(2,128)(2,1)}), bf16[16,1,64]{2,1,0:T(2,128)(2,1)S(1)}, u32[]{:S(2)}, u32[]{:S(2)}) async-start(bf16[16,1,64]{2,1,0:T(2,128)(2,1)} %copy.27), calls=%async_computation | async-start | bytes 16384 | tf_op jit(solution)/shard_map/all_to_all | solution.py:69
  183.0 0.6 select_reduce_fusion.2
  183.6 5.5 %all-to-all-done = bf16[16,1,64]{2,1,0:T(2,128)(2,1)S(1)} async-done(((bf16[16,1,64]{2,1,0:T(2,128)(2,1)}), bf16[16,1,64]{2,1,0:T(2,128)(2,1)S(1)}, u32[]{:S(2)}, u32[]{:S(2)}) %all-to-all-start) | async-done | bytes 2080 | tf_op jit(solution)/shard_map/all_to_all | solution.py:69
  189.1 0.1 reshape.71
  189.2 5.5 %fusion = bf16[1024,3584]{1,0:T(8,128)(2,1)S(1)} fusion(bf16[16,64,3584]{2,1,0:T(8,128)(2,1)} %all-to-all-done.1, f32[1024]{0:T(1024)S(1)} %reshape.71), kind=kLoop, calls=%fused_computation.1 | loop fusion | flops 11010048 | bytes 14684160 | tf_op jit(solution)/shard_map/convert_element_type | solution.py:73
  194.7 0.0 copy-start.1
  194.8 0.0 slice-start
  194.8 9.3 %fusion.14 = f32[1024,3584]{1,0:T(8,128)} fusion(bf16[1024,3584]{1,0:T(8,128)(2,1)S(1)} %fusion, bf16[512,2048]{1,0:T(8,128)(2,1)} %get-tuple-element.11), kind=kOutput, calls=%fused_computation.20 | convolution fusion | flops 3762290688 | bytes 20447232 | tf_op jit(solution)/shard_map/dot_general | solution.py:32
  204.1 0.0 copy-done.1
  204.1 0.0 slice-start.1
  204.1 9.0 %fusion.19 = (bf16[512,1024]{1,0:T(8,128)(2,1)}, bf16[512,1024]{1,0:T(8,128)(2,1)}) fusion(bf16[512,2048]{1,0:T(8,128)(2,1)S(1)} %copy-done.1, bf16[1,1,1024,3584]{3,2,1,0:T(8,128)(2,1)} %param.9, bf16[1024,3584]{1,0:T(8,128)(2,1)S(1)} %fusion), kind=kOutput, calls=%fused_computation.35 | convolution fusion | flops 3765960704 | bytes 15204352 | tf_op jit(solution)/shard_map/dot_general | solution.py:39
  213.1 0.0 slice-done
  213.1 0.0 slice-done.1
  213.1 5.9 %fusion.23 = (bf16[512,1024]{1,0:T(8,128)(2,1)}, bf16[512,1024]{1,0:T(8,128)(2,1)}) fusion(bf16[512,2048]{1,0:T(8,128)(2,1)S(1)} %get-tuple-element.12, bf16[1,1,1024,3584]{3,2,1,0:T(8,128)(2,1)S(1)} %bitcast.71, bf16[1024,3584]{1,0:T(8,128)(2,1)S(1)} %fusion), kind=kOutput, calls=%fused_computation.39 | convolution fusion | flops 3765960704 | bytes 15204352 | tf_op jit(solution)/shard_map/dot_general | solution.py:39
  219.0 9.5 %fusion.11 = bf16[1,1,1024,3584]{3,2,1,0:T(8,128)(2,1)} fusion(f32[1024,3584]{1,0:T(8,128)} %fusion.14, bf16[1024,3584]{1,0:T(8,128)(2,1)S(1)} %fusion, bf16[512,2048]{1,0:T(8,128)(2,1)S(1)} %get-tuple-element.12), kind=kOutput, calls=%fused_computation.16 | convolution fusion | flops 3769630720 | bytes 27787264 | tf_op jit(solution)/shard_map/dot_general | solution.py:32
  228.5 4.7 %maximum_bitcast_fusion = bf16[1,1,1024,2048]{3,2,1,0:T(8,128)(2,1)} fusion(bf16[512,1024]{1,0:T(8,128)(2,1)} %get-tuple-element.10, bf16[512,1024]{1,0:T(8,128)(2,1)} %get-tuple-element.9, bf16[512,1024]{1,0:T(8,128)(2,1)} %get-tuple-element.8, bf16[512,1024]{1,0:T(8,128)(2,1)} %get-tuple-element.7), kind=kLoop, calls=%fused_computation.17 | loop fusion | flops 16777216 | bytes 8388608 | tf_op jit(solution)/shard_map/broadcast_in_dim | solution.py:95
  (8 shorter events, 0.1 us)
Async XLA Ops:
  0.6 23.8 %collective-permute-start = (bf16[1,256,3584]{2,1,0:T(8,128)(2,1)}, bf16[1,256,3584]{2,1,0:T(8,128)(2,1)S(1)}, u32[]{:S(2)}, u32[]{:S(2)}) collective-permute-start(bf16[1,256,3584]{2,1,0:T(8,128)(2,1)} %param.5), channel_id=1, source_target_pairs={{16,0},{32,16},{48,32},{64,48},{80,64},{96,80},{112,96},{0,112},{1... | collective-permute-start | bytes 5505032 | tf_op jit(solution)/shard_map/ppermute | solution.py:10
  29.6 7.8 %copy-start.3 = (bf16[1,256,8]{1,2,0:T(8,128)(2,1)S(1)}, bf16[1,256,8]{1,2,0:T(8,128)(2,1)}, u32[]{:S(2)}) copy-start(bf16[1,256,8]{1,2,0:T(8,128)(2,1)} %param.7) | copy-start | bytes 12292
  29.6 114.6 %all-to-all-start.1 = ((bf16[16,64,3584]{2,1,0:T(8,128)(2,1)}), bf16[16,64,3584]{2,1,0:T(8,128)(2,1)}, u32[]{:S(2)}, u32[]{:S(2)}) async-start(bf16[16,64,3584]{2,1,0:T(8,128)(2,1)} %convolution_convert_fusion), calls=%async_computation.1 | async-start | bytes 14680064 | tf_op jit(solution)/shard_map/all_to_all | solution.py:68
  144.2 5.8 %copy-start = (bf16[512,2048]{1,0:T(8,128)(2,1)S(1)}, bf16[512,2048]{1,0:T(8,128)(2,1)}, u32[]{:S(2)}) copy-start(bf16[512,2048]{1,0:T(8,128)(2,1)} %get-tuple-element.11) | copy-start | bytes 6291460
  157.7 14.1 %copy-start.2 = (s32[1,256,8]{1,2,0:T(8,128)S(1)}, s32[1,256,8]{1,2,0:T(8,128)}, u32[]{:S(2)}) copy-start(s32[1,256,8]{1,2,0:T(8,128)} %param.6) | copy-start | bytes 24580
  166.5 11.6 %all-to-all-start.2 = ((f32[16,1,64]{2,1,0:T(1,128)}), f32[16,1,64]{2,1,0:T(1,128)S(1)}, u32[]{:S(2)}, u32[]{:S(2)}) async-start(f32[16,1,64]{2,1,0:T(1,128)} %bitcast.15), calls=%async_computation.2 | async-start | bytes 16384 | tf_op jit(solution)/shard_map/all_to_all | solution.py:90
  179.3 9.8 %all-to-all-start = ((bf16[16,1,64]{2,1,0:T(2,128)(2,1)}), bf16[16,1,64]{2,1,0:T(2,128)(2,1)S(1)}, u32[]{:S(2)}, u32[]{:S(2)}) async-start(bf16[16,1,64]{2,1,0:T(2,128)(2,1)} %copy.27), calls=%async_computation | async-start | bytes 16384 | tf_op jit(solution)/shard_map/all_to_all | solution.py:69
  194.7 9.4 %copy-start.1 = (bf16[512,2048]{1,0:T(8,128)(2,1)S(1)}, bf16[512,2048]{1,0:T(8,128)(2,1)}, u32[]{:S(2)}) copy-start(bf16[512,2048]{1,0:T(8,128)(2,1)} %get-tuple-element.11) | copy-start | bytes 6291460
  194.8 18.3 %slice-start = ((s8[7340032]{0:T(1024)(128)(4,1)}), s8[4194304]{0:T(1024)(128)(4,1)S(1)}, s32[]{:S(2)}) async-start(s8[7340032]{0:T(1024)(128)(4,1)} %bitcast.70), calls=%async_computation.3 | async-start | bytes 8388608
  204.1 9.0 %slice-start.1 = ((s8[7340032]{0:T(1024)(128)(4,1)}), s8[3145728]{0:T(1024)(128)(4,1)S(1)}, s32[]{:S(2)}) async-start(s8[7340032]{0:T(1024)(128)(4,1)} %bitcast.70), calls=%async_computation.4 | async-start | bytes 6291456
where the time goes:
time: 238 us; the launch traced here: 233 us
  waiting for transfers between devices  135 us (57%)
  matrix products  54.6 us (23%)
  starting transfers between devices  18.1 us (8%)
  other arithmetic  13.5 us (6%)
  local copies, waits for them, and re-layouts  11 us (5%)
    all_to_all x1, waiting for transfers between devices, on_device(): lax.all_to_all(send_rows, 'expert', split_axis=0, concat_axis=0, tiled=True)  103 us
    ppermute x1, waiting for transfers between devices, passed_along(): return lax.ppermute(block, axis, route)  20.8 us
    dot_general x2, matrix products, weight_terms(): lax.dot_general(hidden_rows(gate_up), weighted, (((0,), (0,)), ((), ())),...  18.8 us
    dot_general x2, matrix products, prob_terms(): jnp.dot(hidden_rows(gate_up), weight, preferred_element_type=jnp.float32)  15.8 us
    dot_general x2, matrix products, input_terms(): lax.dot_general(weighted, weight, (((1,), (1,)), ((), ())), preferred_ele...  14.9 us
    all_to_all x1, starting transfers between devices, on_device(): lax.all_to_all(send_rows, 'expert', split_axis=0, concat_axis=0, tiled=True)  7.77 us
    all_to_all x1, waiting for transfers between devices, on_device(): lax.all_to_all(prob_slots.reshape(experts, cap_rows), 'expert', split_axi...  6.32 us
    slice x1, local copies, waits for them, and re-layouts, on_device(): row_grad[first_row:first_row + block_rows]  5.79 us
  transfers between devices with their start and end apart: 4, of which 4 were waited for; matrix products, arithmetic and copies ran while one was open for 3% of the time, Pallas kernels for 0%

commit v1 on v0

v1 whole, which is shorter than its diff:
```python
import functools

import jax
import jax.numpy as jnp
from jax import lax
from jax.experimental import pallas as pl
from jax.experimental.pallas import tpu as pltpu
from jax.sharding import PartitionSpec as P

MESH = pl.DeviceIdType.MESH
F32 = jnp.float32
BF16 = jnp.bfloat16
COLS = 256
LAG = 5


def exchange_kernel(
    grad_hbm,
    route_ref,
    prob_ref,
    pre_hbm,
    weight_hbm,
    hidden_grad,
    down_grad,
    prob_grad,
    shifted,
    line,
    outgoing,
    rows,
    weight,
    pre,
    hidden,
    scaled_t,
    codes,
    picks,
    own_picks,
    prob_tiles,
    back_tile,
    back_tiles,
    row_prob,
    load_sem,
    shift_send,
    shift_recv,
    own_send,
    forward_send,
    line_recv,
    out_send,
    rows_recv,
    code_send,
    code_recv,
    tile_send,
    tile_recv,
    back_send,
    back_recv,
):
    chunks = shifted.shape[0]
    pipe = lax.axis_index("pipe")
    me = lax.axis_index("expert")
    z, x = me // 4, me % 4
    before = lax.rem(pipe + 7, 8)

    def along_x(step):
        return z * 4 + lax.rem(x + step, 4)

    def along_z(step):
        return lax.rem(z + step, 4) * 4 + x

    def first_axis(half, step):
        return along_x(step) * (1 - half) + along_z(step) * half

    def second_axis(half, step):
        return along_z(step) * (1 - half) + along_x(step) * half

    def remote(src, dst, send, recv, device):
        return pltpu.make_async_remote_copy(
            src_ref=src,
            dst_ref=dst,
            send_sem=send,
            recv_sem=recv,
            device_id=device,
            device_id_type=MESH,
        )

    barrier = pltpu.get_barrier_semaphore()
    for step in range(1, 16):
        pl.semaphore_signal(
            barrier, inc=1, device_id=(pipe, lax.rem(me + step, 16)), device_id_type=MESH
        )
    for step in (1, 7):
        pl.semaphore_signal(
            barrier, inc=1, device_id=(lax.rem(pipe + step, 8), me), device_id_type=MESH
        )

    pre_load = pltpu.make_async_copy(pre_hbm, pre, load_sem.at[chunks])
    pre_load.start()

    def weight_load(c):
        return pltpu.make_async_copy(
            weight_hbm.at[:, pl.ds(pl.multiple_of(c * COLS, COLS), COLS)],
            weight.at[c],
            load_sem.at[c],
        )

    @pl.loop(0, chunks)
    def _(c):
        weight_load(c).start()

    expert_iota = lax.broadcasted_iota(jnp.int32, (16, 256), 0)
    member = jnp.zeros((16, 256), F32)
    token_prob = jnp.zeros((16, 256), F32)
    for k in range(8):
        hit = route_ref[k : k + 1, :] == expert_iota
        member = member + jnp.where(hit, 1.0, 0.0)
        token_prob = token_prob + jnp.where(hit, prob_ref[k : k + 1, :].astype(F32), 0.0)
    earlier = (
        lax.broadcasted_iota(jnp.int32, (256, 256), 0)
        <= lax.broadcasted_iota(jnp.int32, (256, 256), 1)
    )
    rank = jnp.dot(
        member.astype(BF16), jnp.where(earlier, 1.0, 0.0).astype(BF16), preferred_element_type=F32
    )
    codes[0] = jnp.where(member > 0.5, rank - 1.0, -1.0)
    slot_iota = lax.broadcasted_iota(jnp.int32, (64, 256), 0).astype(F32)
    for e in range(16):
        own_picks[e * 64 : e * 64 + 64, :] = jnp.where(
            codes[0, e : e + 1, :] == slot_iota, 1.0, 0.0
        ).astype(BF16)
    diagonal = (
        lax.broadcasted_iota(jnp.int32, (16, 1024), 1) // 64
        == lax.broadcasted_iota(jnp.int32, (16, 1024), 0)
    )
    slot_probs = lax.dot_general(
        token_prob.astype(BF16),
        own_picks[...],
        (((1,), (1,)), ((), ())),
        preferred_element_type=F32,
    )
    slot_probs = jnp.sum(jnp.where(diagonal, slot_probs, 0.0), axis=0, keepdims=True)
    for r in range(8):
        prob_tiles[me, r : r + 1, :] = slot_probs[:, r * 128 : r * 128 + 128]

    pl.semaphore_wait(barrier, 17)

    def shift_copy(c):
        return remote(
            grad_hbm.at[:, pl.ds(pl.multiple_of(c * COLS, COLS), COLS)],
            shifted.at[c],
            shift_send.at[c],
            shift_recv.at[c],
            (before, me),
        )

    @pl.loop(0, chunks)
    def _(c):
        shift_copy(c).start()

    code_copies = []
    for half, towards in ((0, along_x), (1, along_z)):
        for slot, step in ((1, 1), (2, 3), (3, 2)):
            index = half * 3 + slot
            code_copies.append(
                remote(
                    codes.at[0],
                    codes.at[index],
                    code_send.at[index - 1],
                    code_recv.at[index - 1],
                    (pipe, towards(step)),
                )
            )
    for copy in code_copies:
        copy.start()

    def tile_copy(step):
        return remote(
            prob_tiles.at[me],
            prob_tiles.at[me],
            tile_send.at[step],
            tile_recv.at[step],
            (pipe, lax.rem(me + step, 16)),
        )

    @pl.loop(1, 16)
    def _(step):
        tile_copy(step).start()

    def own_copy(c, side):
        half = lax.rem(c, 2)
        return remote(
            shifted.at[c],
            line.at[c, side],
            own_send.at[c, side],
            line_recv.at[c, side],
            (pipe, first_axis(half, 1 if side == 0 else 3)),
        )

    def forward_copy(c, side):
        half = lax.rem(c, 2)
        part = pl.ds(side * 128, 128)
        return remote(
            line.at[c, side, part],
            line.at[c, 2, part],
            forward_send.at[c, side],
            line_recv.at[c, 2 + side],
            (pipe, first_axis(half, 1 if side == 0 else 3)),
        )

    def out_copy(c, step, half):
        target = rows.at[c, z] if half == 0 else rows.at[c, :, x]
        return remote(
            outgoing.at[c, step - 1],
            target,
            out_send.at[c, step - 1],
            rows_recv.at[c, step - 1],
            (pipe, second_axis(half, step)),
        )

    def send_own(c):
        shift_copy(c).wait_recv()
        own_copy(c, 0).start()
        own_copy(c, 1).start()

    def forward(c):
        own_copy(c, 0).wait_recv()
        forward_copy(c, 0).start()
        own_copy(c, 1).wait_recv()
        forward_copy(c, 1).start()

    def build_picks():
        for copy in code_copies:
            copy.wait_recv()
        for half, towards in ((0, along_z), (1, along_x)):
            for source in range(4):
                index = 0 if source == 0 else half * 3 + source
                for step in range(4):
                    code = codes[index, pl.ds(towards(step), 1), :]
                    picks[half, source, step * 64 : step * 64 + 64, :] = jnp.where(
                        code == slot_iota, 1.0, 0.0
                    ).astype(BF16)

    def pick_and_send(c):
        half = lax.rem(c, 2)
        forward_copy(c, 0).wait_recv()
        forward_copy(c, 1).wait_recv()
        mine = x * (1 - half) + z * half
        for source, delta in ((0, 0), (1, 3), (2, 1), (3, 2)):
            block = shifted[c] if source == 0 else line[c, source - 1]
            place = lax.rem(mine + delta, 4)
            picked = jnp.dot(picks[half, source], block, preferred_element_type=F32).astype(BF16)
            for step in range(1, 4):
                outgoing[c, step - 1, place] = picked[step * 64 : step * 64 + 64]
            rows[c, z * (1 - half) + place * half, place * (1 - half) + x * half] = picked[:64]
        for h in range(2):

            @pl.when(half == h)
            def _():
                for step in range(1, 4):
                    out_copy(c, step, h).start()

    def activate():
        pre_load.wait()

        @pl.loop(1, 16)
        def _(step):
            tile_copy(step).wait_recv()

        mine = prob_tiles[:, pl.ds(me // 2, 1), :].reshape(16, 128)
        mine = jnp.where(lax.rem(me, 2) == 1, pltpu.roll(mine, 64, 1), mine)
        turned = jnp.concatenate([mine] * 8, axis=0).T
        for j in range(16):
            row_prob[j * 64 : j * 64 + 64, :] = jnp.broadcast_to(
                turned[:64, j : j + 1], (64, 128)
            )

        @pl.loop(0, 8)
        def _(b):
            here = pl.ds(pl.multiple_of(b * 128, 128), 128)
            factor = row_prob[here, :]
            for q in range(8):
                gate = pre[here, q * 128 : q * 128 + 128].astype(F32)
                up = pre[here, 1024 + q * 128 : 1024 + q * 128 + 128].astype(F32)
                value = gate * jax.nn.sigmoid(gate) * up
                hidden[here, q * 128 : q * 128 + 128] = value.astype(BF16)
                scaled_t[q * 128 : q * 128 + 128, here] = (value * factor).T.astype(BF16)

        hidden_grad[...] = jnp.zeros_like(hidden_grad)

    def arrived(c):
        for step in range(1, 4):
            out_copy(c, step, 0).wait_recv()

    def add_input_terms(c):
        weight_load(c).wait()

        @pl.loop(0, 4)
        def _(b):
            here = pl.ds(pl.multiple_of(b * 256, 256), 256)
            hidden_grad[here, :] += lax.dot_general(
                rows[c, b].reshape(256, COLS),
                weight[c],
                (((1,), (1,)), ((), ())),
                preferred_element_type=F32,
            )

    def weight_terms(c):
        there = pl.ds(pl.multiple_of(c * COLS, COLS), COLS)
        block = rows[c].reshape(1024, COLS)

        @pl.loop(0, 4)
        def _(b):
            here = pl.ds(pl.multiple_of(b * 256, 256), 256)
            down_grad[here, there] = jnp.dot(
                scaled_t[here, :], block, preferred_element_type=F32
            ).astype(BF16)

    @pl.loop(0, chunks + LAG)
    def _(i):
        @pl.when(i < chunks)
        def _():
            send_own(i)

        @pl.when((i >= 1) & (i < chunks + 1))
        def _():
            forward(i - 1)

        @pl.when(i == 1)
        def _():
            build_picks()

        @pl.when((i >= 2) & (i < chunks + 2))
        def _():
            pick_and_send(i - 2)

        @pl.when(i == 2)
        def _():
            activate()

        @pl.when(i >= LAG)
        def _():
            arrived(i - LAG)
            add_input_terms(i - LAG)

            @pl.when(i < chunks + LAG - 1)
            def _():
                weight_terms(i - LAG)

    @pl.loop(0, 8)
    def _(b):
        here = pl.ds(pl.multiple_of(b * 128, 128), 128)
        factor = row_prob[here, :]
        total = jnp.zeros((128, 128), F32)
        for q in range(8):
            value = hidden_grad[here, q * 128 : q * 128 + 128]
            total = total + hidden[here, q * 128 : q * 128 + 128].astype(F32) * value
            hidden_grad[here, q * 128 : q * 128 + 128] = value * factor
        back_tile[pl.ds(b, 1), :] = jnp.sum(total.T, axis=0, keepdims=True)

    def back_copy(step):
        return remote(
            back_tile,
            back_tiles.at[me],
            back_send.at[step],
            back_recv.at[step],
            (pipe, lax.rem(me + step, 16)),
        )

    @pl.loop(1, 16)
    def _(step):
        back_copy(step).start()

    back_tiles[me] = back_tile[...]
    weight_terms(chunks - 1)

    @pl.loop(1, 16)
    def _(step):
        back_copy(step).wait_recv()

    mine = back_tiles[:, pl.ds(me // 2, 1), :].reshape(16, 128)
    other = pltpu.roll(mine, 64, 1)
    low = lax.broadcasted_iota(jnp.int32, (16, 128), 1) < 64
    odd = lax.rem(me, 2) == 1
    both = jnp.where(low == jnp.logical_not(odd), mine, other)
    spread = jnp.where(diagonal, jnp.concatenate([both] * 8, axis=1), 0.0)
    high = spread.astype(BF16)
    rest = spread - high.astype(F32)
    middle = rest.astype(BF16)
    small = (rest - middle.astype(F32)).astype(BF16)
    pieces = jnp.dot(
        jnp.concatenate([high, middle, small], axis=0), own_picks[...], preferred_element_type=F32
    )
    token_grad = pieces[:16] + pieces[16:32] + pieces[32:]
    result = jnp.zeros((8, 256), F32)
    for e in range(16):
        result = result + jnp.where(route_ref[...] == e, token_grad[e : e + 1, :], 0.0)
    prob_grad[...] = result

    for copy in code_copies:
        copy.wait_send()

    @pl.loop(1, 16)
    def _(step):
        tile_copy(step).wait_send()
        back_copy(step).wait_send()

    @pl.loop(0, chunks)
    def _(c):
        shift_copy(c).wait_send()
        for side in range(2):
            own_copy(c, side).wait_send()
            forward_copy(c, side).wait_send()
        for step in range(1, 4):
            out_copy(c, step, 0).wait_send()


def exchange(grad, route_t, prob_t, pre, weight):
    chunks = grad.shape[1] // COLS
    hbm = pl.BlockSpec(memory_space=pl.ANY)
    vmem = pl.BlockSpec(memory_space=pltpu.VMEM)
    dma = pltpu.SemaphoreType.DMA
    return pl.pallas_call(
        exchange_kernel,
        out_shape=(
            jax.ShapeDtypeStruct((1024, 1024), F32),
            jax.ShapeDtypeStruct((1024, chunks * COLS), BF16),
            jax.ShapeDtypeStruct((8, 256), F32),
        ),
        in_specs=[hbm, vmem, vmem, hbm, hbm],
        out_specs=(vmem, vmem, vmem),
        scratch_shapes=[
            pltpu.VMEM((chunks, 256, COLS), BF16),
            pltpu.VMEM((chunks, 3, 256, COLS), BF16),
            pltpu.VMEM((chunks, 3, 4, 64, COLS), BF16),
            pltpu.VMEM((chunks, 4, 4, 64, COLS), BF16),
            pltpu.VMEM((chunks, 1024, COLS), BF16),
            pltpu.VMEM((1024, 2048), BF16),
            pltpu.VMEM((1024, 1024), BF16),
            pltpu.VMEM((1024, 1024), BF16),
            pltpu.VMEM((7, 16, 256), F32),
            pltpu.VMEM((2, 4, 256, 256), BF16),
            pltpu.VMEM((1024, 256), BF16),
            pltpu.VMEM((16, 8, 128), F32),
            pltpu.VMEM((8, 128), F32),
            pltpu.VMEM((16, 8, 128), F32),
            pltpu.VMEM((1024, 128), F32),
            dma((chunks + 1,)),
            dma((chunks,)),
            dma((chunks,)),
            dma((chunks, 2)),
            dma((chunks, 2)),
            dma((chunks, 4)),
            dma((chunks, 3)),
            dma((chunks, 3)),
            dma((6,)),
            dma((6,)),
            dma((16,)),
            dma((16,)),
            dma((16,)),
            dma((16,)),
        ],
        compiler_params=pltpu.CompilerParams(
            collective_id=0, has_side_effects=True, vmem_limit_bytes=62 * 2**20
        ),
        name="exchange",
    )(grad, route_t, prob_t, pre, weight)


def input_grad_kernel(hidden_grad, pre, out):
    half = pre.shape[1] // 2
    gate = pre[:, :half].astype(F32)
    up = pre[:, half:].astype(F32)
    sig = jax.nn.sigmoid(gate)
    grad = hidden_grad[...]
    out[:, :half] = (grad * up * sig * (1.0 + gate * (1.0 - sig))).astype(BF16)
    out[:, half:] = (grad * (gate * sig)).astype(BF16)


def input_grad(hidden_grad, pre):
    block = 128
    return pl.pallas_call(
        input_grad_kernel,
        out_shape=jax.ShapeDtypeStruct(pre.shape, BF16),
        grid=(pre.shape[0] // block,),
        in_specs=[
            pl.BlockSpec((block, pre.shape[1] // 2), lambda i: (i, 0)),
            pl.BlockSpec((block, pre.shape[1]), lambda i: (i, 0)),
        ],
        out_specs=pl.BlockSpec((block, pre.shape[1]), lambda i: (i, 0)),
        name="input_grad",
    )(hidden_grad, pre)


def on_device(boundary_grad, route_ids, route_probs, saved_preact, down_weight):
    pre = saved_preact[0, 0]
    hidden_grad, down_grad, prob_grad = exchange(
        boundary_grad[0], route_ids[0].T, route_probs[0].T, pre, down_weight[0, 0]
    )
    return (input_grad(hidden_grad, pre)[None, None], down_grad[None, None], prob_grad.T[None])


def solution(mesh):
    placed = (
        P("pipe", "expert", None),
        P("pipe", "expert", None),
        P("pipe", "expert", None),
        P("pipe", "expert", None, None),
        P("pipe", "expert", None, None),
    )
    return jax.shard_map(
        on_device,
        mesh=mesh,
        in_specs=placed,
        out_specs=(
            P("pipe", "expert", None, None),
            P("pipe", "expert", None, None),
            P("pipe", "expert", None),
        ),
        check_vma=False,
    )
```

time: 238 us -> 132 us (0.55)
  the two profiles are of different devices: /device:TPU:1 before, /device:TPU:0 now
where the time goes in v1:
time: 132 us
  Pallas kernels  124 us (94%)
  local copies, waits for them, and re-layouts  7.22 us (5%)
    pallas_call x1, Pallas kernels, exchange(): pl.pallas_call(exchange_kernel, out_shape=(jax.ShapeDtypeStruct((1024, 10...  116 us
    pallas_call x1, Pallas kernels, input_grad(): pl.pallas_call(input_grad_kernel, out_shape=jax.ShapeDtypeStruct(pre.shap...  8.17 us
    unnamed x4, local copies, waits for them, and re-layouts  7.22 us

profile of v1, /device:TPU:0, one launch (start us, length us, event | category | flops | bytes accessed | tf_op | source)
XLA Modules:
  0.0 132.1 jit_solution(13735587298459200064)
XLA Ops:
  0.6 116.1 %exchange.1 = (f32[1024,1024]{1,0:T(8,128)}, bf16[1024,3584]{1,0:T(8,128)(2,1)}, f32[8,256]{1,0:T(8,128)}) custom-call(bf16[256,3584]{1,0:T(8,128)(2,1)} %bitcast.19, s32[8,256]{1,0:T(8,128)} %bitcast.21, bf16[8,256]{1,0:T(8,128)(2,1)} %bitcast.22, bf16[1024,2048]{1,0:T(8,128)(2,1)} %bitcast.14, bf16[1024,3584]{1,0:T(8,128)(2,1)} %bitcast.17), custom_call_target="tpu_custom_call" | custom-call | tf_op jit(solution)/shard_map/exchange/pallas_call | solution.py:419
  116.7 8.2 %input_grad.1 = bf16[1024,2048]{1,0:T(8,128)(2,1)} custom-call(f32[1024,1024]{1,0:T(8,128)} %get-tuple-element.6.hidden_grad, bf16[1024,2048]{1,0:T(8,128)(2,1)} %bitcast.15), custom_call_target="tpu_custom_call" | custom-call | tf_op jit(solution)/shard_map/input_grad/pallas_call | solution.py:478
  124.9 0.0 copy-start
  124.9 6.6 %copy.10 = bf16[1,1,1024,3584]{3,2,1,0:T(8,128)(2,1)} copy(bf16[1,1,1024,3584]{3,2,1,0:T(8,128)(2,1)} %bitcast.16) | data formatting | bytes 14680064
  131.5 0.0 copy-done
  131.5 0.6 copy.11
Async XLA Ops:
  124.9 6.6 %copy-start = (f32[8,256]{1,0:T(8,128)S(1)}, f32[8,256]{1,0:T(8,128)}, u32[]{:S(2)}) copy-start(f32[8,256]{1,0:T(8,128)} %get-tuple-element.8) | copy-start | bytes 24580

commit v2 on v1

--- a/solution.py
+++ b/solution.py
@@ -11,7 +11,10 @@
 F32 = jnp.float32
 BF16 = jnp.bfloat16
 COLS = 256
-LAG = 5
+SHIFTS = 4
+FORWARD_LAG = 3
+PICK_LAG = 6
+LAG = 10
 
 
 def exchange_kernel(
@@ -20,15 +23,15 @@
     prob_ref,
     pre_hbm,
     weight_hbm,
-    hidden_grad,
+    pre,
     down_grad,
     prob_grad,
+    hidden_grad,
     shifted,
     line,
     outgoing,
     rows,
     weight,
-    pre,
     hidden,
     scaled_t,
     codes,
@@ -150,7 +153,7 @@
             (before, me),
         )
 
-    @pl.loop(0, chunks)
+    @pl.loop(0, SHIFTS)
     def _(c):
         shift_copy(c).start()
 
@@ -216,6 +219,11 @@
 
     def send_own(c):
         shift_copy(c).wait_recv()
+
+        @pl.when(c + SHIFTS < chunks)
+        def _():
+            shift_copy(c + SHIFTS).start()
+
         own_copy(c, 0).start()
         own_copy(c, 1).start()
 
@@ -278,7 +286,13 @@
             for q in range(8):
                 gate = pre[here, q * 128 : q * 128 + 128].astype(F32)
                 up = pre[here, 1024 + q * 128 : 1024 + q * 128 + 128].astype(F32)
-                value = gate * jax.nn.sigmoid(gate) * up
+                sig = jax.nn.sigmoid(gate)
+                silu = gate * sig
+                value = silu * up
+                pre[here, q * 128 : q * 128 + 128] = (
+                    up * sig * (1.0 + gate * (1.0 - sig))
+                ).astype(BF16)
+                pre[here, 1024 + q * 128 : 1024 + q * 128 + 128] = silu.astype(BF16)
                 hidden[here, q * 128 : q * 128 + 128] = value.astype(BF16)
                 scaled_t[q * 128 : q * 128 + 128, here] = (value * factor).T.astype(BF16)
 
@@ -318,21 +332,18 @@
         def _():
             send_own(i)
 
-        @pl.when((i >= 1) & (i < chunks + 1))
+        @pl.when((i >= FORWARD_LAG) & (i < chunks + FORWARD_LAG))
         def _():
-            forward(i - 1)
-
-        @pl.when(i == 1)
+            forward(i - FORWARD_LAG)
+
+        @pl.when(i == PICK_LAG - 1)
         def _():
             build_picks()
-
-        @pl.when((i >= 2) & (i < chunks + 2))
+            activate()
+
+        @pl.when((i >= PICK_LAG) & (i < chunks + PICK_LAG))
         def _():
-            pick_and_send(i - 2)
-
-        @pl.when(i == 2)
-        def _():
-            activate()
+            pick_and_send(i - PICK_LAG)
 
         @pl.when(i >= LAG)
         def _():
@@ -351,7 +362,6 @@
         for q in range(8):
             value = hidden_grad[here, q * 128 : q * 128 + 128]
             total = total + hidden[here, q * 128 : q * 128 + 128].astype(F32) * value
-            hidden_grad[here, q * 128 : q * 128 + 128] = value * factor
         back_tile[pl.ds(b, 1), :] = jnp.sum(total.T, axis=0, keepdims=True)
 
     def back_copy(step):
@@ -369,6 +379,17 @@
 
     back_tiles[me] = back_tile[...]
     weight_terms(chunks - 1)
+
+    @pl.loop(0, 8)
+    def _(b):
+        here = pl.ds(pl.multiple_of(b * 128, 128), 128)
+        factor = row_prob[here, :]
+        for q in range(8):
+            value = hidden_grad[here, q * 128 : q * 128 + 128] * factor
+            for first in (q * 128, 1024 + q * 128):
+                pre[here, first : first + 128] = (
+                    value * pre[here, first : first + 128].astype(F32)
+                ).astype(BF16)
 
     @pl.loop(1, 16)
     def _(step):
@@ -419,19 +440,19 @@
     return pl.pallas_call(
         exchange_kernel,
         out_shape=(
-            jax.ShapeDtypeStruct((1024, 1024), F32),
-            jax.ShapeDtypeStruct((1024, chunks * COLS), BF16),
-            jax.ShapeDtypeStruct((8, 256), F32),
+            pltpu.VMEM((1024, 2048), BF16),
+            pltpu.VMEM((1024, chunks * COLS), BF16),
+            pltpu.VMEM((8, 256), F32),
         ),
         in_specs=[hbm, vmem, vmem, hbm, hbm],
         out_specs=(vmem, vmem, vmem),
         scratch_shapes=[
+            pltpu.VMEM((1024, 1024), F32),
             pltpu.VMEM((chunks, 256, COLS), BF16),
             pltpu.VMEM((chunks, 3, 256, COLS), BF16),
             pltpu.VMEM((chunks, 3, 4, 64, COLS), BF16),
             pltpu.VMEM((chunks, 4, 4, 64, COLS), BF16),
             pltpu.VMEM((chunks, 1024, COLS), BF16),
-            pltpu.VMEM((1024, 2048), BF16),
             pltpu.VMEM((1024, 1024), BF16),
             pltpu.VMEM((1024, 1024), BF16),
             pltpu.VMEM((7, 16, 256), F32),
@@ -457,43 +478,46 @@
             dma((16,)),
         ],
         compiler_params=pltpu.CompilerParams(
-            collective_id=0, has_side_effects=True, vmem_limit_bytes=62 * 2**20
+            collective_id=0, has_side_effects=True, vmem_limit_bytes=50 * 2**20
         ),
         name="exchange",
     )(grad, route_t, prob_t, pre, weight)
 
 
-def input_grad_kernel(hidden_grad, pre, out):
-    half = pre.shape[1] // 2
-    gate = pre[:, :half].astype(F32)
-    up = pre[:, half:].astype(F32)
-    sig = jax.nn.sigmoid(gate)
-    grad = hidden_grad[...]
-    out[:, :half] = (grad * up * sig * (1.0 + gate * (1.0 - sig))).astype(BF16)
-    out[:, half:] = (grad * (gate * sig)).astype(BF16)
-
-
-def input_grad(hidden_grad, pre):
-    block = 128
+def store_kernel(*refs):
+    count = len(refs) // 2
+    copies = [
+        pltpu.make_async_copy(refs[i], refs[count + i], refs[-1].at[i]) for i in range(count)
+    ]
+    for copy in copies:
+        copy.start()
+    for copy in copies:
+        copy.wait()
+
+
+def store(*results):
     return pl.pallas_call(
-        input_grad_kernel,
-        out_shape=jax.ShapeDtypeStruct(pre.shape, BF16),
-        grid=(pre.shape[0] // block,),
-        in_specs=[
-            pl.BlockSpec((block, pre.shape[1] // 2), lambda i: (i, 0)),
-            pl.BlockSpec((block, pre.shape[1]), lambda i: (i, 0)),
-        ],
-        out_specs=pl.BlockSpec((block, pre.shape[1]), lambda i: (i, 0)),
-        name="input_grad",
-    )(hidden_grad, pre)
+        store_kernel,
+        out_shape=tuple(jax.ShapeDtypeStruct(r.shape, r.dtype) for r in results),
+        in_specs=[pl.BlockSpec(memory_space=pltpu.VMEM)] * len(results),
+        out_specs=tuple(pl.BlockSpec(memory_space=pl.ANY) for _ in results),
+        scratch_shapes=[pltpu.SemaphoreType.DMA((len(results),))],
+        compiler_params=pltpu.CompilerParams(vmem_limit_bytes=2**20),
+        name="store",
+    )(*(pltpu.with_memory_space_constraint(r, pltpu.VMEM) for r in results))
 
 
 def on_device(boundary_grad, route_ids, route_probs, saved_preact, down_weight):
-    pre = saved_preact[0, 0]
-    hidden_grad, down_grad, prob_grad = exchange(
-        boundary_grad[0], route_ids[0].T, route_probs[0].T, pre, down_weight[0, 0]
-    )
-    return (input_grad(hidden_grad, pre)[None, None], down_grad[None, None], prob_grad.T[None])
+    preact_grad, down_grad, prob_grad = store(
+        *exchange(
+            boundary_grad[0],
+            route_ids[0].T,
+            route_probs[0].T,
+            saved_preact[0, 0],
+            down_weight[0, 0],
+        )
+    )
+    return (preact_grad[None, None], down_grad[None, None], prob_grad.T[None])
 
 
 def solution(mesh):

time: 132 us -> 103 us (0.78)
  the two profiles are of different devices: /device:TPU:0 before, /device:TPU:1 now
where the time goes in v2:
time: 103 us
  Pallas kernels  103 us (100%)
    pallas_call x1, Pallas kernels, exchange(): pl.pallas_call(exchange_kernel, out_shape=(pltpu.VMEM((1024, 2048), BF16)...  98.1 us
    pallas_call x1, Pallas kernels, store(): pl.pallas_call(store_kernel, out_shape=tuple((jax.ShapeDtypeStruct(r.shap...  4.46 us

profile of v2, /device:TPU:1, one launch (start us, length us, event | category | flops | bytes accessed | tf_op | source)
XLA Modules:
  0.0 103.2 jit_solution(17094215844261669383)
XLA Ops:
  0.6 98.1 %exchange.1 = (bf16[1024,2048]{1,0:T(8,128)(2,1)S(1)}, bf16[1024,3584]{1,0:T(8,128)(2,1)S(1)}, f32[8,256]{1,0:T(8,128)S(1)}) custom-call(bf16[256,3584]{1,0:T(8,128)(2,1)} %bitcast.16, s32[8,256]{1,0:T(8,128)} %bitcast.17, bf16[8,256]{1,0:T(8,128)(2,1)} %bitcast.18, bf16[1024,2048]{1,0:T(8,128)(2,1)} %bitcast.15, bf16[1024,3584]{1,0:T(8,128)(2,1)} %bitcast.14), custom_call_target="tpu_custom_call" | custom-call | tf_op jit(solution)/shard_map/exchange/pallas_call | solution.py:440
  98.7 4.5 %store.1 = (bf16[1024,2048]{1,0:T(8,128)(2,1)}, bf16[1024,3584]{1,0:T(8,128)(2,1)}, f32[8,256]{1,0:T(8,128)}) custom-call(bf16[1024,2048]{1,0:T(8,128)(2,1)S(1)} %get-tuple-element.9.refs_0_, bf16[1024,3584]{1,0:T(8,128)(2,1)S(1)} %get-tuple-element.10.refs_1_, f32[8,256]{1,0:T(8,128)S(1)} %get-tuple-element.11.refs_2_), custom_call_target="tpu_custom_call" | custom-call | tf_op jit(solution)/shard_map/store/pallas_call | solution.py:499

commit v3 on v2

--- a/solution.py
+++ b/solution.py
@@ -14,18 +14,20 @@
 SHIFTS = 4
 FORWARD_LAG = 3
 PICK_LAG = 6
-LAG = 10
+LAG = 9
 
 
 def exchange_kernel(
     grad_hbm,
-    route_ref,
-    prob_ref,
+    route_hbm,
+    prob_hbm,
     pre_hbm,
     weight_hbm,
     pre,
     down_grad,
     prob_grad,
+    route_ref,
+    prob_ref,
     hidden_grad,
     shifted,
     line,
@@ -94,6 +96,12 @@
             barrier, inc=1, device_id=(lax.rem(pipe + step, 8), me), device_id_type=MESH
         )
 
+    small_loads = (
+        pltpu.make_async_copy(route_hbm, route_ref, load_sem.at[chunks + 1]),
+        pltpu.make_async_copy(prob_hbm, prob_ref, load_sem.at[chunks + 2]),
+    )
+    for load in small_loads:
+        load.start()
     pre_load = pltpu.make_async_copy(pre_hbm, pre, load_sem.at[chunks])
     pre_load.start()
 
@@ -107,6 +115,24 @@
     @pl.loop(0, chunks)
     def _(c):
         weight_load(c).start()
+
+    pl.semaphore_wait(barrier, 17)
+
+    def shift_copy(c):
+        return remote(
+            grad_hbm.at[:, pl.ds(pl.multiple_of(c * COLS, COLS), COLS)],
+            shifted.at[c],
+            shift_send.at[c],
+            shift_recv.at[c],
+            (before, me),
+        )
+
+    @pl.loop(0, SHIFTS)
+    def _(c):
+        shift_copy(c).start()
+
+    for load in small_loads:
+        load.wait()
 
     expert_iota = lax.broadcasted_iota(jnp.int32, (16, 256), 0)
     member = jnp.zeros((16, 256), F32)
@@ -141,21 +167,6 @@
     slot_probs = jnp.sum(jnp.where(diagonal, slot_probs, 0.0), axis=0, keepdims=True)
     for r in range(8):
         prob_tiles[me, r : r + 1, :] = slot_probs[:, r * 128 : r * 128 + 128]
-
-    pl.semaphore_wait(barrier, 17)
-
-    def shift_copy(c):
-        return remote(
-            grad_hbm.at[:, pl.ds(pl.multiple_of(c * COLS, COLS), COLS)],
-            shifted.at[c],
-            shift_send.at[c],
-            shift_recv.at[c],
-            (before, me),
-        )
-
-    @pl.loop(0, SHIFTS)
-    def _(c):
-        shift_copy(c).start()
 
     code_copies = []
     for half, towards in ((0, along_x), (1, along_z)):
@@ -264,7 +275,7 @@
                 for step in range(1, 4):
                     out_copy(c, step, h).start()
 
-    def activate():
+    def spread_probs():
         pre_load.wait()
 
         @pl.loop(1, 16)
@@ -279,7 +290,10 @@
                 turned[:64, j : j + 1], (64, 128)
             )
 
-        @pl.loop(0, 8)
+        hidden_grad[...] = jnp.zeros_like(hidden_grad)
+
+    def activate(first):
+        @pl.loop(first, first + 2)
         def _(b):
             here = pl.ds(pl.multiple_of(b * 128, 128), 128)
             factor = row_prob[here, :]
@@ -296,8 +310,6 @@
                 hidden[here, q * 128 : q * 128 + 128] = value.astype(BF16)
                 scaled_t[q * 128 : q * 128 + 128, here] = (value * factor).T.astype(BF16)
 
-        hidden_grad[...] = jnp.zeros_like(hidden_grad)
-
     def arrived(c):
         for step in range(1, 4):
             out_copy(c, step, 0).wait_recv()
@@ -305,26 +317,18 @@
     def add_input_terms(c):
         weight_load(c).wait()
 
-        @pl.loop(0, 4)
-        def _(b):
-            here = pl.ds(pl.multiple_of(b * 256, 256), 256)
-            hidden_grad[here, :] += lax.dot_general(
-                rows[c, b].reshape(256, COLS),
-                weight[c],
-                (((1,), (1,)), ((), ())),
-                preferred_element_type=F32,
-            )
+        hidden_grad[...] += lax.dot_general(
+            rows[c].reshape(1024, COLS),
+            weight[c],
+            (((1,), (1,)), ((), ())),
+            preferred_element_type=F32,
+        )
 
     def weight_terms(c):
         there = pl.ds(pl.multiple_of(c * COLS, COLS), COLS)
-        block = rows[c].reshape(1024, COLS)
-
-        @pl.loop(0, 4)
-        def _(b):
-            here = pl.ds(pl.multiple_of(b * 256, 256), 256)
-            down_grad[here, there] = jnp.dot(
-                scaled_t[here, :], block, preferred_element_type=F32
-            ).astype(BF16)
+        down_grad[:, there] = jnp.dot(
+            scaled_t[...], rows[c].reshape(1024, COLS), preferred_element_type=F32
+        ).astype(BF16)
 
     @pl.loop(0, chunks + LAG)
     def _(i):
@@ -339,7 +343,14 @@
         @pl.when(i == PICK_LAG - 1)
         def _():
             build_picks()
-            activate()
+
+        @pl.when(i == 3)
+        def _():
+            spread_probs()
+
+        @pl.when((i >= 4) & (i < 8))
+        def _():
+            activate(2 * i - 8)
 
         @pl.when((i >= PICK_LAG) & (i < chunks + PICK_LAG))
         def _():
@@ -444,9 +455,11 @@
             pltpu.VMEM((1024, chunks * COLS), BF16),
             pltpu.VMEM((8, 256), F32),
         ),
-        in_specs=[hbm, vmem, vmem, hbm, hbm],
+        in_specs=[hbm] * 5,
         out_specs=(vmem, vmem, vmem),
         scratch_shapes=[
+            pltpu.VMEM((8, 256), jnp.int32),
+            pltpu.VMEM((8, 256), BF16),
             pltpu.VMEM((1024, 1024), F32),
             pltpu.VMEM((chunks, 256, COLS), BF16),
             pltpu.VMEM((chunks, 3, 256, COLS), BF16),
@@ -462,7 +475,7 @@
             pltpu.VMEM((8, 128), F32),
             pltpu.VMEM((16, 8, 128), F32),
             pltpu.VMEM((1024, 128), F32),
-            dma((chunks + 1,)),
+            dma((chunks + 3,)),
             dma((chunks,)),
             dma((chunks,)),
             dma((chunks, 2)),

time: 103 us -> 98.3 us (0.954)
  Pallas kernels: 103 us -> 97.6 us
    pallas_call x1, Pallas kernels: 98.1 us -> 93.1 us  [exchange(): pl.pallas_call(exchange_kernel, out_shape=(pltpu.VMEM((1024, 2048), BF16)...]
where the time goes in v3:
time: 98.3 us; the launch traced here: 98.2 us
  Pallas kernels  97.6 us (99%)
    pallas_call x1, Pallas kernels, exchange(): pl.pallas_call(exchange_kernel, out_shape=(pltpu.VMEM((1024, 2048), BF16)...  93.1 us
    pallas_call x1, Pallas kernels, store(): pl.pallas_call(store_kernel, out_shape=tuple((jax.ShapeDtypeStruct(r.shap...  4.46 us

profile of v3, /device:TPU:1, one launch (start us, length us, event | category | flops | bytes accessed | tf_op | source)
XLA Modules:
  0.0 98.2 jit_solution(14312880655100821622)
XLA Ops:
  0.6 93.1 %exchange.1 = (bf16[1024,2048]{1,0:T(8,128)(2,1)S(1)}, bf16[1024,3584]{1,0:T(8,128)(2,1)S(1)}, f32[8,256]{1,0:T(8,128)S(1)}) custom-call(bf16[256,3584]{1,0:T(8,128)(2,1)} %bitcast.16, s32[8,256]{1,0:T(8,128)} %bitcast.17, bf16[8,256]{1,0:T(8,128)(2,1)} %bitcast.18, bf16[1024,2048]{1,0:T(8,128)(2,1)} %bitcast.15, bf16[1024,3584]{1,0:T(8,128)(2,1)} %bitcast.14), custom_call_target="tpu_custom_call" | custom-call | tf_op jit(solution)/shard_map/exchange/pallas_call | solution.py:451
  93.8 4.5 %store.1 = (bf16[1024,2048]{1,0:T(8,128)(2,1)}, bf16[1024,3584]{1,0:T(8,128)(2,1)}, f32[8,256]{1,0:T(8,128)}) custom-call(bf16[1024,2048]{1,0:T(8,128)(2,1)S(1)} %get-tuple-element.9.refs_0_, bf16[1024,3584]{1,0:T(8,128)(2,1)S(1)} %get-tuple-element.10.refs_1_, f32[8,256]{1,0:T(8,128)S(1)} %get-tuple-element.11.refs_2_), custom_call_target="tpu_custom_call" | custom-call | tf_op jit(solution)/shard_map/store/pallas_call | solution.py:512

commit v4 on v3

--- a/solution.py
+++ b/solution.py
@@ -15,6 +15,7 @@
 FORWARD_LAG = 3
 PICK_LAG = 6
 LAG = 9
+DEFERRED = 2
 
 
 def exchange_kernel(
@@ -25,7 +26,8 @@
     weight_hbm,
     pre,
     down_grad,
-    prob_grad,
+    back,
+    own_picks,
     route_ref,
     prob_ref,
     hidden_grad,
@@ -38,7 +40,6 @@
     scaled_t,
     codes,
     picks,
-    own_picks,
     prob_tiles,
     back_tile,
     back_tiles,
@@ -361,7 +362,7 @@
             arrived(i - LAG)
             add_input_terms(i - LAG)
 
-            @pl.when(i < chunks + LAG - 1)
+            @pl.when(i < chunks + LAG - DEFERRED)
             def _():
                 weight_terms(i - LAG)
 
@@ -389,7 +390,9 @@
         back_copy(step).start()
 
     back_tiles[me] = back_tile[...]
-    weight_terms(chunks - 1)
+    @pl.loop(chunks - DEFERRED, chunks)
+    def _(c):
+        weight_terms(c)
 
     @pl.loop(0, 8)
     def _(b):
@@ -410,20 +413,7 @@
     other = pltpu.roll(mine, 64, 1)
     low = lax.broadcasted_iota(jnp.int32, (16, 128), 1) < 64
     odd = lax.rem(me, 2) == 1
-    both = jnp.where(low == jnp.logical_not(odd), mine, other)
-    spread = jnp.where(diagonal, jnp.concatenate([both] * 8, axis=1), 0.0)
-    high = spread.astype(BF16)
-    rest = spread - high.astype(F32)
-    middle = rest.astype(BF16)
-    small = (rest - middle.astype(F32)).astype(BF16)
-    pieces = jnp.dot(
-        jnp.concatenate([high, middle, small], axis=0), own_picks[...], preferred_element_type=F32
-    )
-    token_grad = pieces[:16] + pieces[16:32] + pieces[32:]
-    result = jnp.zeros((8, 256), F32)
-    for e in range(16):
-        result = result + jnp.where(route_ref[...] == e, token_grad[e : e + 1, :], 0.0)
-    prob_grad[...] = result
+    back[...] = jnp.where(low == jnp.logical_not(odd), mine, other)
 
     for copy in code_copies:
         copy.wait_send()
@@ -453,12 +443,13 @@
         out_shape=(
             pltpu.VMEM((1024, 2048), BF16),
             pltpu.VMEM((1024, chunks * COLS), BF16),
-            pltpu.VMEM((8, 256), F32),
+            pltpu.VMEM((16, 128), F32),
+            pltpu.VMEM((1024, 256), BF16),
+            pltpu.VMEM((8, 256), jnp.int32),
         ),
         in_specs=[hbm] * 5,
-        out_specs=(vmem, vmem, vmem),
+        out_specs=(vmem,) * 5,
         scratch_shapes=[
-            pltpu.VMEM((8, 256), jnp.int32),
             pltpu.VMEM((8, 256), BF16),
             pltpu.VMEM((1024, 1024), F32),
             pltpu.VMEM((chunks, 256, COLS), BF16),
@@ -470,7 +461,6 @@
             pltpu.VMEM((1024, 1024), BF16),
             pltpu.VMEM((7, 16, 256), F32),
             pltpu.VMEM((2, 4, 256, 256), BF16),
-            pltpu.VMEM((1024, 256), BF16),
             pltpu.VMEM((16, 8, 128), F32),
             pltpu.VMEM((8, 128), F32),
             pltpu.VMEM((16, 8, 128), F32),
@@ -497,31 +487,58 @@
     )(grad, route_t, prob_t, pre, weight)
 
 
-def store_kernel(*refs):
-    count = len(refs) // 2
+def finish_kernel(
+    preact_in, down_in, back, own_picks, routes, preact_out, down_out, prob_out, result_ref, sem
+):
     copies = [
-        pltpu.make_async_copy(refs[i], refs[count + i], refs[-1].at[i]) for i in range(count)
+        pltpu.make_async_copy(down_in, down_out, sem.at[0]),
+        pltpu.make_async_copy(preact_in, preact_out, sem.at[1]),
     ]
     for copy in copies:
         copy.start()
+    diagonal = (
+        lax.broadcasted_iota(jnp.int32, (16, 1024), 1) // 64
+        == lax.broadcasted_iota(jnp.int32, (16, 1024), 0)
+    )
+    spread = jnp.where(diagonal, jnp.concatenate([back[...]] * 8, axis=1), 0.0)
+    high = spread.astype(BF16)
+    rest = spread - high.astype(F32)
+    middle = rest.astype(BF16)
+    small = (rest - middle.astype(F32)).astype(BF16)
+    pieces = jnp.dot(
+        jnp.concatenate([high, middle, small], axis=0), own_picks[...], preferred_element_type=F32
+    )
+    token_grad = pieces[:16] + pieces[16:32] + pieces[32:]
+    result = jnp.zeros((8, 256), F32)
+    for e in range(16):
+        result = result + jnp.where(routes[...] == e, token_grad[e : e + 1, :], 0.0)
+    result_ref[...] = result
+    copies.append(pltpu.make_async_copy(result_ref, prob_out, sem.at[2]))
+    copies[2].start()
     for copy in copies:
         copy.wait()
 
 
-def store(*results):
+def finish(preact_grad, down_grad, back, own_picks, routes):
+    shape = jax.ShapeDtypeStruct
+    results = (preact_grad, down_grad, back, own_picks, routes)
     return pl.pallas_call(
-        store_kernel,
-        out_shape=tuple(jax.ShapeDtypeStruct(r.shape, r.dtype) for r in results),
-        in_specs=[pl.BlockSpec(memory_space=pltpu.VMEM)] * len(results),
-        out_specs=tuple(pl.BlockSpec(memory_space=pl.ANY) for _ in results),
-        scratch_shapes=[pltpu.SemaphoreType.DMA((len(results),))],
-        compiler_params=pltpu.CompilerParams(vmem_limit_bytes=2**20),
-        name="store",
+        finish_kernel,
+        out_shape=(
+            shape(preact_grad.shape, BF16),
+            shape(down_grad.shape, BF16),
+            shape(routes.shape, F32),
+        ),
+        in_specs=[pl.BlockSpec(memory_space=pltpu.VMEM)] * 5,
+        out_specs=(pl.BlockSpec(memory_space=pl.ANY),) * 3,
+        scratch_shapes=[pltpu.VMEM(routes.shape, F32), pltpu.SemaphoreType.DMA((3,))],
+        compiler_params=pltpu.CompilerParams(vmem_limit_bytes=2 * 2**20),
+        name="finish",
     )(*(pltpu.with_memory_space_constraint(r, pltpu.VMEM) for r in results))
 
 
 def on_device(boundary_grad, route_ids, route_probs, saved_preact, down_weight):
-    preact_grad, down_grad, prob_grad = store(
+    preact_grad, down_grad, prob_grad = finish(
         *exchange(
             boundary_grad[0],
             route_ids[0].T,

time: 98.3 us -> 98 us (level)
  no operation moved by 1% of the time
where the time goes in v4:
time: 98 us; the launch traced here: 97.9 us
  Pallas kernels  97.2 us (99%)
    pallas_call x1, Pallas kernels, exchange(): pl.pallas_call(exchange_kernel, out_shape=(pltpu.VMEM((1024, 2048), BF16)...  92.7 us
    pallas_call x1, Pallas kernels, finish(): pl.pallas_call(finish_kernel, out_shape=(shape(preact_grad.shape, BF16),...  4.47 us

profile of v4, /device:TPU:1, one launch (start us, length us, event | category | flops | bytes accessed | tf_op | source)
XLA Modules:
  0.0 97.9 jit_solution(2052384700466469322)
XLA Ops:
  0.6 92.7 %exchange.1 = (bf16[1024,2048]{1,0:T(8,128)(2,1)S(1)}, bf16[1024,3584]{1,0:T(8,128)(2,1)S(1)}, f32[16,128]{1,0:T(8,128)S(1)}, bf16[1024,256]{1,0:T(8,128)(2,1)S(1)}, s32[8,256]{1,0:T(8,128)S(1)}) custom-call(bf16[256,3584]{1,0:T(8,128)(2,1)} %bitcast.16, s32[8,256]{1,0:T(8,128)} %bitcast.17, bf16[8,256]{1,0:T(8,128)(2,1)} %bitcast.18, ...), custom_call_target="tpu_custom_call" | custom-call | tf_op jit(solution)/shard_map/exchange/pallas_call | solution.py:441
  93.4 4.5 %finish.1 = (bf16[1024,2048]{1,0:T(8,128)(2,1)}, bf16[1024,3584]{1,0:T(8,128)(2,1)}, f32[8,256]{1,0:T(8,128)}) custom-call(bf16[1024,2048]{1,0:T(8,128)(2,1)S(1)} %get-tuple-element.11.preact_in, bf16[1024,3584]{1,0:T(8,128)(2,1)S(1)} %get-tuple-element.12.down_in, f32[16,128]{1,0:T(8,128)S(1)} %get-tuple-element.13.back, ...), custom_call_target="tpu_custom_call" | custom-call | tf_op jit(solution)/shard_map/finish/pallas_call | solution.py:525

commit v5 on v4

--- a/solution.py
+++ b/solution.py
@@ -273,7 +273,7 @@
 
             @pl.when(half == h)
             def _():
-                for step in range(1, 4):
+                for step in (2, 1, 3):
                     out_copy(c, step, h).start()
 
     def spread_probs():

time: 98 us -> 97.4 us (level)
  no operation moved by 1% of the time
where the time goes in v5:
time: 97.4 us; the launch traced here: 97.2 us
  Pallas kernels  96.6 us (99%)
    pallas_call x1, Pallas kernels, exchange(): pl.pallas_call(exchange_kernel, out_shape=(pltpu.VMEM((1024, 2048), BF16)...  92.1 us
    pallas_call x1, Pallas kernels, finish(): pl.pallas_call(finish_kernel, out_shape=(shape(preact_grad.shape, BF16),...  4.47 us

profile of v5, /device:TPU:1, one launch (start us, length us, event | category | flops | bytes accessed | tf_op | source)
XLA Modules:
  0.0 97.2 jit_solution(14903659701524693048)
XLA Ops:
  0.6 92.1 %exchange.1 = (bf16[1024,2048]{1,0:T(8,128)(2,1)S(1)}, bf16[1024,3584]{1,0:T(8,128)(2,1)S(1)}, f32[16,128]{1,0:T(8,128)S(1)}, bf16[1024,256]{1,0:T(8,128)(2,1)S(1)}, s32[8,256]{1,0:T(8,128)S(1)}) custom-call(bf16[256,3584]{1,0:T(8,128)(2,1)} %bitcast.16, s32[8,256]{1,0:T(8,128)} %bitcast.17, bf16[8,256]{1,0:T(8,128)(2,1)} %bitcast.18, ...), custom_call_target="tpu_custom_call" | custom-call | tf_op jit(solution)/shard_map/exchange/pallas_call | solution.py:441
  92.8 4.5 %finish.1 = (bf16[1024,2048]{1,0:T(8,128)(2,1)}, bf16[1024,3584]{1,0:T(8,128)(2,1)}, f32[8,256]{1,0:T(8,128)}) custom-call(bf16[1024,2048]{1,0:T(8,128)(2,1)S(1)} %get-tuple-element.11.preact_in, bf16[1024,3584]{1,0:T(8,128)(2,1)S(1)} %get-tuple-element.12.down_in, f32[16,128]{1,0:T(8,128)S(1)} %get-tuple-element.13.back, ...), custom_call_target="tpu_custom_call" | custom-call | tf_op jit(solution)/shard_map/finish/pallas_call | solution.py:525

commit v6 on v5

--- a/solution.py
+++ b/solution.py
@@ -333,13 +333,13 @@
 
     @pl.loop(0, chunks + LAG)
     def _(i):
+        @pl.when((i >= FORWARD_LAG) & (i < chunks + FORWARD_LAG))
+        def _():
+            forward(i - FORWARD_LAG)
+
         @pl.when(i < chunks)
         def _():
             send_own(i)
-
-        @pl.when((i >= FORWARD_LAG) & (i < chunks + FORWARD_LAG))
-        def _():
-            forward(i - FORWARD_LAG)
 
         @pl.when(i == PICK_LAG - 1)
         def _():

time: 97.4 us -> 99.2 us (1.018)
  Pallas kernels: 96.6 us -> 98.5 us
    pallas_call x1, Pallas kernels: 92.1 us -> 94 us  [exchange(): pl.pallas_call(exchange_kernel, out_shape=(pltpu.VMEM((1024, 2048), BF16)...]
where the time goes in v6:
time: 99.2 us; the launch traced here: 99.1 us
  Pallas kernels  98.5 us (99%)
    pallas_call x1, Pallas kernels, exchange(): pl.pallas_call(exchange_kernel, out_shape=(pltpu.VMEM((1024, 2048), BF16)...  94 us
    pallas_call x1, Pallas kernels, finish(): pl.pallas_call(finish_kernel, out_shape=(shape(preact_grad.shape, BF16),...  4.47 us

profile of v6, /device:TPU:1, one launch (start us, length us, event | category | flops | bytes accessed | tf_op | source)
XLA Modules:
  0.0 99.1 jit_solution(10633914801084326559)
XLA Ops:
  0.6 94.0 %exchange.1 = (bf16[1024,2048]{1,0:T(8,128)(2,1)S(1)}, bf16[1024,3584]{1,0:T(8,128)(2,1)S(1)}, f32[16,128]{1,0:T(8,128)S(1)}, bf16[1024,256]{1,0:T(8,128)(2,1)S(1)}, s32[8,256]{1,0:T(8,128)S(1)}) custom-call(bf16[256,3584]{1,0:T(8,128)(2,1)} %bitcast.16, s32[8,256]{1,0:T(8,128)} %bitcast.17, bf16[8,256]{1,0:T(8,128)(2,1)} %bitcast.18, ...), custom_call_target="tpu_custom_call" | custom-call | tf_op jit(solution)/shard_map/exchange/pallas_call | solution.py:441
  94.7 4.5 %finish.1 = (bf16[1024,2048]{1,0:T(8,128)(2,1)}, bf16[1024,3584]{1,0:T(8,128)(2,1)}, f32[8,256]{1,0:T(8,128)}) custom-call(bf16[1024,2048]{1,0:T(8,128)(2,1)S(1)} %get-tuple-element.11.preact_in, bf16[1024,3584]{1,0:T(8,128)(2,1)S(1)} %get-tuple-element.12.down_in, f32[16,128]{1,0:T(8,128)S(1)} %get-tuple-element.13.back, ...), custom_call_target="tpu_custom_call" | custom-call | tf_op jit(solution)/shard_map/finish/pallas_call | solution.py:525
